TPU v7x, 256 devices: a whole 4x4x8 slice. The times are simulated.
256 devices in a mesh: ta: 8 (over x, core), xyz: 32 (over y, z).
Axes of the slice: x: 4, y: 4, z: 8, core: 2. Of those that a mesh axis runs over, the one named last changes fastest.
Arguments:
- nulls: bfloat16 [32, 128, 32, 16, 128], P('ta', 'xyz'), may hold values from -1.1953125 to 1.1953125
- time_links: bfloat16 [16, 128, 32, 64, 128], P('ta', 'xyz'), may hold values from -0.5 to 0.5
- space_links: bfloat16 [32, 64, 32, 64, 128], P('ta', 'xyz'), may hold values from -0.5 to 0.5
- owner_lists: int32 [32, 64], replicated, may hold values from -1 to 1023, as said below
Outputs:
- coarse_links: float32 [8, 2048, 1024], P('ta', 'xyz')
Inputs may be any that keep to these rules, and one draw needn't show every extreme that they name: `owner_lists`: row d lists, in increasing order, the aggregates that shard d owns, followed by -1 in the remaining slots; each of the 1024 aggregate ids appears exactly once. Exactly half of the shards own 64 aggregates each and the others none. The 32 aggregates with ids q * 32 to q * 32 + 31 belong to exactly 8 owners, 4 to each.
All inputs are finite; a program needn't handle non-finite values.
Results may differ from a plain program's by a relative error of at most 0.0029.
Values may be sent and summed in bfloat16 or wider, within the bound.
A program may use at most 64 MiB of HBM per device.

v0:
```python
import jax
import jax.numpy as jnp
from jax import lax
from jax.sharding import PartitionSpec as P


def shifted(array, axis, by):
    count = lax.axis_size(axis)
    return lax.ppermute(array, axis, [(i, (i + by) % count) for i in range(count)])


def forward_image(link_mats, upper_nulls):
    half_width = link_mats.shape[-2]
    upper_real = upper_nulls[..., :half_width]
    upper_imag = upper_nulls[..., half_width:]
    paired = jnp.stack(
        [
            jnp.concatenate([upper_real, -upper_imag], axis=-1),
            jnp.concatenate([upper_imag, upper_real], axis=-1),
        ],
        axis=-3,
    )
    image_pair = jnp.einsum(
        "...ik,...pnk->...pni", link_mats, paired, preferred_element_type=jnp.float32
    )
    joined = jnp.concatenate([image_pair[..., 0, :, :], image_pair[..., 1, :, :]], axis=-1)
    return joined.astype(jnp.bfloat16)


def conjugate_pair(lower_nulls):
    half_width = lower_nulls.shape[-1] // 2
    turned = jnp.concatenate(
        [-lower_nulls[..., half_width:], lower_nulls[..., :half_width]], axis=-1
    )
    return jnp.stack([lower_nulls, turned], axis=-3)


def on_device(nulls, time_links, space_links, owner_lists):
    time_rows, space_rows, side_rows, vectors, doubled = nulls.shape
    time_aggs = time_rows // 2
    space_aggs = space_rows // 2
    side_aggs = side_rows // 4
    local_count = time_aggs * space_aggs * side_aggs
    edge_time = shifted(nulls[0:1], "ta", -1)
    upper_time = jnp.concatenate([nulls[2::2], edge_time], axis=0)
    edge_space = shifted(nulls[:, 0:1], "xyz", -1)
    upper_space = jnp.concatenate([nulls[:, 2::2], edge_space], axis=1)
    image_time = forward_image(time_links, upper_time).reshape(
        time_aggs, space_aggs, 2, side_aggs, 4, vectors, doubled
    )
    pair_time = conjugate_pair(nulls[1::2]).reshape(
        time_aggs, space_aggs, 2, side_aggs, 4, 2, vectors, doubled
    )
    block_time = jnp.einsum(
        "txcaypnk,txcaymk->txapnm", pair_time, image_time, preferred_element_type=jnp.float32
    )
    image_space = forward_image(space_links, upper_space).reshape(
        time_aggs, 2, space_aggs, side_aggs, 4, vectors, doubled
    )
    pair_space = conjugate_pair(nulls[:, 1::2]).reshape(
        time_aggs, 2, space_aggs, side_aggs, 4, 2, vectors, doubled
    )
    block_space = jnp.einsum(
        "tcxaypnk,tcxaymk->txapnm", pair_space, image_space, preferred_element_type=jnp.float32
    )
    block_width = 2 * vectors * vectors
    link_rows = jnp.concatenate(
        [
            block_time.reshape(local_count, block_width),
            block_space.reshape(local_count, block_width),
        ],
        axis=1,
    )
    shard_index = lax.axis_index("xyz")
    my_list = lax.dynamic_index_in_dim(owner_lists, shard_index, 0, keepdims=False)
    present = my_list >= 0
    everything = lax.all_gather(link_rows, "xyz", axis=0, tiled=True)
    picked = everything[jnp.maximum(my_list, 0)]
    result = jnp.where(present[:, None], picked, 0.0)
    return result[None]


def solution(mesh):
    return jax.shard_map(
        on_device,
        mesh=mesh,
        in_specs=(
            P("ta", "xyz", None, None, None),
            P("ta", "xyz", None, None, None),
            P("ta", "xyz", None, None, None),
            P(),
        ),
        out_specs=P("ta", "xyz", None),
        check_vma=False,
    )
```

profile of v0, /device:TPU:2, one launch (start us, length us, event | category | flops | bytes accessed | tf_op | source)
XLA Modules:
  0.0 130.2 jit_solution(7621202235726365997)
XLA Ops:
  6.5 1.5 %fusion.37 = (bf16[1,4,32,16,128]{4,3,2,1,0:T(8,128)(2,1)S(1)}, bf16[1,4,32,16,128]{4,3,2,1,0:T(8,128)(2,1)S(1)}) fusion(bf16[4,4,32,16,128]{4,3,2,1,0:T(8,128)(2,1)} %param.4), kind=kLoop, calls=%fused_computation.48 | loop fusion | bytes 2097152 | tf_op jit(solution)/shard_map/slice | solution.py:45
  8.4 1.2 fusion.39
  9.6 8.3 %collective-permute-start.1 = (bf16[4,1,32,16,128]{4,3,2,1,0:T(8,128)(2,1)}, bf16[4,1,32,16,128]{4,3,2,1,0:T(8,128)(2,1)}, u32[]{:S(2)}, u32[]{:S(2)}) collective-permute-start(bf16[4,1,32,16,128]{4,3,2,1,0:T(8,128)(2,1)} %get-tuple-element.12), channel_id=1, source_target_pairs={{0,31},{1,0},{2,1},{3,2},{4,3},{5,4},{6,5},{7,6},{8,7},{9,8},{10,9... | collective-permute-start | bytes 1572872 | tf_op jit(solution)/shard_map/ppermute | solution.py:9
  18.7 0.6 pad_maximum_fusion.4
  19.7 0.6 pad_maximum_fusion.5
  20.3 0.7 fusion.34
  21.1 1.2 maximum_bitcast_fusion
  22.2 1.0 copy-done.1
  23.3 2.3 %fusion.14 = bf16[2,4,32,2,16,64]{5,4,3,2,1,0:T(8,128)(2,1)S(1)} fusion(bf16[2,4,32,64,128]{4,3,2,1,0:T(8,128)(2,1)S(1)} %copy-done.1, bf16[2,4,32,1,16,128]{5,4,3,2,1,0:T(8,128)(2,1)S(1)} %get-tuple-element.14, bf16[2,4,32,1,16,128]{5,4,3,2,1,0:T(8,128)(2,1)S(1)} %get-tuple-element.13), kind=kOutput, calls=%fused_computation.17 | convolution fusion | flops 135790592 | bytes 7340032 | tf_op jit(solution)/shard_map/...ik,...pnk->...pni/dot_general | solution.py:23
  25.5 0.6 fusion.36
  26.1 1.0 fusion.24
  27.4 2.3 %collective-permute-done.1 = bf16[4,1,32,16,128]{4,3,2,1,0:T(8,128)(2,1)} collective-permute-done((bf16[4,1,32,16,128]{4,3,2,1,0:T(8,128)(2,1)}, bf16[4,1,32,16,128]{4,3,2,1,0:T(8,128)(2,1)}, u32[]{:S(2)}, u32[]{:S(2)}) %collective-permute-start.1) | collective-permute-done | bytes 524320 | tf_op jit(solution)/shard_map/ppermute | solution.py:9
  29.7 1.9 %fusion.35 = (bf16[4,2,32,16,64]{4,3,2,1,0:T(8,128)(2,1)S(1)}, bf16[4,2,32,16,64]{4,3,2,1,0:T(8,128)(2,1)S(1)}, bf16[4,2,32,16,64]{4,3,2,1,0:T(8,128)(2,1)S(1)}) fusion(bf16[4,1,32,16,128]{4,3,2,1,0:T(8,128)(2,1)} %collective-permute-done.1, bf16[4,1,32,16,128]{4,3,2,1,0:T(8,128)(2,1)S(1)} %copy-done.3), kind=kLoop, calls=%fused_computation.46 | loop fusion | flops 2621440 | bytes 2621440 | tf_op jit(solution)/shard_map/neg | solution.py:18
  31.7 1.2 maximum_bitcast_fusion.3
  32.8 1.0 copy-done.2
  33.9 2.3 %fusion.19 = bf16[4,2,32,2,16,64]{5,4,3,2,1,0:T(8,128)(2,1)S(1)} fusion(bf16[4,2,32,64,128]{4,3,2,1,0:T(8,128)(2,1)S(1)} %copy-done.2, bf16[4,2,32,1,16,128]{5,4,3,2,1,0:T(8,128)(2,1)S(1)} %get-tuple-element.21, bf16[4,2,32,1,16,128]{5,4,3,2,1,0:T(8,128)(2,1)S(1)} %get-tuple-element.20), kind=kOutput, calls=%fused_computation.18 | convolution fusion | flops 135790592 | bytes 7340032 | tf_op jit(solution)/shard_map/...ik,...pnk->...pni/dot_general | solution.py:23
  36.1 0.6 fusion.38
  36.7 1.0 fusion.27
  38.0 0.7 pad_maximum_fusion.6
  38.7 0.7 maximum_bitcast_fusion.6
  39.4 0.7 compare_bitcast_fusion
  40.1 79.5 %all-gather.2.cloned.1.call-done = f32[1024,1024]{1,0:T(8,128)} async-done(((f32[32,1024]{1,0:T(8,128)}), f32[1024,1024]{1,0:T(8,128)}) %all-gather.2.cloned.1.call-update) | async-done | bytes 4194320 | tf_op jit(solution)/shard_map/all_gather | solution.py:77
  119.6 3.0 %gather_fusion = f32[64,1024]{1,0:T(8,128)S(1)} fusion(f32[1024,1024]{1,0:T(8,128)} %all-gather.2.cloned.1.call-done, s32[1024]{0:T(1024)S(1)} %pad_clamp_fusion), kind=kCustom, calls=%fused_computation | custom fusion | bytes 524544 | tf_op jit(solution)/shard_map/gather | solution.py:78
  122.5 0.8 bitcast_select_fusion
  (17 shorter events, 2.2 us)
Async XLA Ops:
  6.5 1.9 %copy-start = (bf16[4,4,32,16,128]{4,3,2,1,0:T(8,128)(2,1)S(1)}, bf16[4,4,32,16,128]{4,3,2,1,0:T(8,128)(2,1)}, u32[]{:S(2)}) copy-start(bf16[4,4,32,16,128]{4,3,2,1,0:T(8,128)(2,1)} %param.4) | copy-start | bytes 6291460
  6.5 113.0 %all-gather.2.cloned.1.call-start = ((), (), s32[]{:S(2)}) async-start(), calls=%async_computation | async-start | bytes 4325376 | tf_op jit(solution)/shard_map/all_gather | solution.py:77
  8.1 12.3 %collective-permute-start = (bf16[1,4,32,16,128]{4,3,2,1,0:T(8,128)(2,1)S(1)}, bf16[1,4,32,16,128]{4,3,2,1,0:T(8,128)(2,1)S(1)}, u32[]{:S(2)}, u32[]{:S(2)}) collective-permute-start(bf16[1,4,32,16,128]{4,3,2,1,0:T(8,128)(2,1)S(1)} %get-tuple-element.8), channel_id=1, source_target_pairs={{0,224},{32,0},{64,32},{96,64},{128,96},{160,128},{192,160},{224,1... | collective-permute-start | bytes 1572872 | tf_op jit(solution)/shard_map/ppermute | solution.py:9
  9.6 20.1 %collective-permute-start.1 = (bf16[4,1,32,16,128]{4,3,2,1,0:T(8,128)(2,1)}, bf16[4,1,32,16,128]{4,3,2,1,0:T(8,128)(2,1)}, u32[]{:S(2)}, u32[]{:S(2)}) collective-permute-start(bf16[4,1,32,16,128]{4,3,2,1,0:T(8,128)(2,1)} %get-tuple-element.12), channel_id=1, source_target_pairs={{0,31},{1,0},{2,1},{3,2},{4,3},{5,4},{6,5},{7,6},{8,7},{9,8},{10,9... | collective-permute-start | bytes 1572872 | tf_op jit(solution)/shard_map/ppermute | solution.py:9
  21.1 2.2 %copy-start.1 = (bf16[2,4,32,64,128]{4,3,2,1,0:T(8,128)(2,1)S(1)}, bf16[2,4,32,64,128]{4,3,2,1,0:T(8,128)(2,1)}, u32[]{:S(2)}) copy-start(bf16[2,4,32,64,128]{4,3,2,1,0:T(8,128)(2,1)} %param.5) | copy-start | bytes 12582916
  26.1 3.6 %copy-start.3 = (bf16[4,1,32,16,128]{4,3,2,1,0:T(8,128)(2,1)S(1)}, bf16[4,1,32,16,128]{4,3,2,1,0:T(8,128)(2,1)}, u32[]{:S(2)}) copy-start(bf16[4,1,32,16,128]{4,3,2,1,0:T(8,128)(2,1)} %get-tuple-element.11) | copy-start | bytes 1572868
  31.7 2.2 %copy-start.2 = (bf16[4,2,32,64,128]{4,3,2,1,0:T(8,128)(2,1)S(1)}, bf16[4,2,32,64,128]{4,3,2,1,0:T(8,128)(2,1)}, u32[]{:S(2)}) copy-start(bf16[4,2,32,64,128]{4,3,2,1,0:T(8,128)(2,1)} %param.6) | copy-start | bytes 12582916
Sparse Core Ops, SparseCore 0:
  38.8 80.7 all-gather.1
where the time goes:
time: 130 us
  waiting for transfers between devices  81.8 us (63%)
  between operations  13.5 us (10%)
  local copies, waits for them, and re-layouts  10.1 us (8%)
  other arithmetic  9.83 us (8%)
  starting transfers between devices  8.33 us (6%)
  matrix products  6.58 us (5%)
    all_gather x1, waiting for transfers between devices, on_device(): everything = lax.all_gather(link_rows, 'xyz', axis=0, tiled=True)  79.5 us
    ppermute x2, starting transfers between devices, shifted(): lax.ppermute(array, axis, [(i, (i + by) % count) for i in range(count)])  8.32 us
    dot_general x2, matrix products, forward_image(): jnp.einsum('...ik,...pnk->...pni', link_mats, paired, preferred_element_t...  4.55 us
    gather x1, local copies, waits for them, and re-layouts, on_device(): picked = everything[jnp.maximum(my_list, 0)]  2.98 us
    neg x2, other arithmetic, forward_image(): -upper_imag  2.63 us
  transfers between devices with their start and end apart: 3, of which 2 were waited for; matrix products, arithmetic and copies ran while one was open for 8% of the time, Pallas kernels for 0%

commit v1 on v0

--- a/solution.py
+++ b/solution.py
@@ -74,7 +74,8 @@
     shard_index = lax.axis_index("xyz")
     my_list = lax.dynamic_index_in_dim(owner_lists, shard_index, 0, keepdims=False)
     present = my_list >= 0
-    everything = lax.all_gather(link_rows, "xyz", axis=0, tiled=True)
+    sent = jnp.stack([link_rows] * lax.axis_size("xyz"))
+    everything = jnp.concatenate(lax.all_to_all(sent, "xyz", 0, 0), axis=0)
     picked = everything[jnp.maximum(my_list, 0)]
     result = jnp.where(present[:, None], picked, 0.0)
     return result[None]

time: 130 us -> 142 us (1.092)
  waiting for transfers between devices: 81.8 us -> 97.5 us
  between operations: 13.5 us -> 0.17 us
  starting transfers between devices: 8.33 us -> 15.9 us
  local copies, waits for them, and re-layouts: 10.1 us -> 12.4 us
    all_to_all x0 -> x1, waiting for transfers between devices: none -> 95.1 us  [on_device(): everything = jnp.concatenate(lax.all_to_all(sent, 'xyz', 0, 0), axis=0)]
    all_gather x1 -> x0, waiting for transfers between devices: 79.5 us -> none  [on_device(): everything = lax.all_gather(link_rows, 'xyz', axis=0, tiled=True)]
    all_to_all x0 -> x1, starting transfers between devices: none -> 7.59 us  [on_device(): everything = jnp.concatenate(lax.all_to_all(sent, 'xyz', 0, 0), axis=0)]
    another operation x0 -> x1, local copies, waits for them, and re-layouts: none -> 2.51 us  [on_device(): sent = jnp.stack([link_rows] * lax.axis_size('xyz'))]
where the time goes in v1:
time: 142 us
  waiting for transfers between devices  97.5 us (69%)
  starting transfers between devices  15.9 us (11%)
  local copies, waits for them, and re-layouts  12.4 us (9%)
  other arithmetic  9.22 us (6%)
  matrix products  6.58 us (5%)
    all_to_all x1, waiting for transfers between devices, on_device(): everything = jnp.concatenate(lax.all_to_all(sent, 'xyz', 0, 0), axis=0)  95.1 us
    ppermute x2, starting transfers between devices, shifted(): lax.ppermute(array, axis, [(i, (i + by) % count) for i in range(count)])  8.32 us
    all_to_all x1, starting transfers between devices, on_device(): everything = jnp.concatenate(lax.all_to_all(sent, 'xyz', 0, 0), axis=0)  7.59 us
    dot_general x2, matrix products, forward_image(): jnp.einsum('...ik,...pnk->...pni', link_mats, paired, preferred_element_t...  4.55 us
    gather x1, local copies, waits for them, and re-layouts, on_device(): picked = everything[jnp.maximum(my_list, 0)]  2.98 us
  transfers between devices with their start and end apart: 3, of which 2 were waited for; matrix products, arithmetic and copies ran while one was open for 8% of the time, Pallas kernels for 0%

profile of v1, /device:TPU:2, one launch (start us, length us, event | category | flops | bytes accessed | tf_op | source)
XLA Modules:
  0.0 141.7 jit_solution(1060848002997325754)
XLA Ops:
  0.0 1.5 %fusion.37 = (bf16[1,4,32,16,128]{4,3,2,1,0:T(8,128)(2,1)S(1)}, bf16[1,4,32,16,128]{4,3,2,1,0:T(8,128)(2,1)S(1)}) fusion(bf16[4,4,32,16,128]{4,3,2,1,0:T(8,128)(2,1)} %param.4), kind=kLoop, calls=%fused_computation.48 | loop fusion | bytes 2097152 | tf_op jit(solution)/shard_map/slice | solution.py:45
  1.9 1.0 fusion.39
  2.9 8.3 %collective-permute-start.1 = (bf16[4,1,32,16,128]{4,3,2,1,0:T(8,128)(2,1)}, bf16[4,1,32,16,128]{4,3,2,1,0:T(8,128)(2,1)}, u32[]{:S(2)}, u32[]{:S(2)}) collective-permute-start(bf16[4,1,32,16,128]{4,3,2,1,0:T(8,128)(2,1)} %get-tuple-element.12), channel_id=1, source_target_pairs={{0,31},{1,0},{2,1},{3,2},{4,3},{5,4},{6,5},{7,6},{8,7},{9,8},{10,9... | collective-permute-start | bytes 1572872 | tf_op jit(solution)/shard_map/ppermute | solution.py:9
  12.0 0.6 pad_maximum_fusion.4
  13.0 0.6 pad_maximum_fusion.5
  13.6 0.7 fusion.34
  14.4 1.2 maximum_bitcast_fusion
  15.5 1.0 copy-done.1
  16.5 2.3 %fusion.14 = bf16[2,4,32,2,16,64]{5,4,3,2,1,0:T(8,128)(2,1)S(1)} fusion(bf16[2,4,32,64,128]{4,3,2,1,0:T(8,128)(2,1)S(1)} %copy-done.1, bf16[2,4,32,1,16,128]{5,4,3,2,1,0:T(8,128)(2,1)S(1)} %get-tuple-element.14, bf16[2,4,32,1,16,128]{5,4,3,2,1,0:T(8,128)(2,1)S(1)} %get-tuple-element.13), kind=kOutput, calls=%fused_computation.17 | convolution fusion | flops 135790592 | bytes 7340032 | tf_op jit(solution)/shard_map/...ik,...pnk->...pni/dot_general | solution.py:23
  18.8 0.6 fusion.36
  19.4 1.0 fusion.24
  20.7 2.3 %collective-permute-done.1 = bf16[4,1,32,16,128]{4,3,2,1,0:T(8,128)(2,1)} collective-permute-done((bf16[4,1,32,16,128]{4,3,2,1,0:T(8,128)(2,1)}, bf16[4,1,32,16,128]{4,3,2,1,0:T(8,128)(2,1)}, u32[]{:S(2)}, u32[]{:S(2)}) %collective-permute-start.1) | collective-permute-done | bytes 524320 | tf_op jit(solution)/shard_map/ppermute | solution.py:9
  23.0 2.0 %fusion.35 = (bf16[4,2,32,16,64]{4,3,2,1,0:T(8,128)(2,1)S(1)}, bf16[4,2,32,16,64]{4,3,2,1,0:T(8,128)(2,1)S(1)}, bf16[4,2,32,16,64]{4,3,2,1,0:T(8,128)(2,1)S(1)}) fusion(bf16[4,1,32,16,128]{4,3,2,1,0:T(8,128)(2,1)} %collective-permute-done.1, bf16[4,1,32,16,128]{4,3,2,1,0:T(8,128)(2,1)S(1)} %get-tuple-element.11), kind=kLoop, calls=%fused_computation.46 | loop fusion | flops 2621440 | bytes 2621440 | tf_op jit(solution)/shard_map/neg | solution.py:18
  25.0 1.2 maximum_bitcast_fusion.3
  26.2 1.0 copy-done.2
  27.2 2.3 %fusion.19 = bf16[4,2,32,2,16,64]{5,4,3,2,1,0:T(8,128)(2,1)S(1)} fusion(bf16[4,2,32,64,128]{4,3,2,1,0:T(8,128)(2,1)S(1)} %copy-done.2, bf16[4,2,32,1,16,128]{5,4,3,2,1,0:T(8,128)(2,1)S(1)} %get-tuple-element.21, bf16[4,2,32,1,16,128]{5,4,3,2,1,0:T(8,128)(2,1)S(1)} %get-tuple-element.20), kind=kOutput, calls=%fused_computation.18 | convolution fusion | flops 135790592 | bytes 7340032 | tf_op jit(solution)/shard_map/...ik,...pnk->...pni/dot_general | solution.py:23
  30.0 1.0 fusion.27
  31.3 2.5 %stack.38 = f32[32,32,1024]{2,1,0:T(8,128)} broadcast(f32[32,1024]{1,0:T(8,128)S(1)} %pad_maximum_fusion.6), dimensions={1,2} | broadcast | bytes 4325376 | tf_op jit(solution)/shard_map/stack | solution.py:77
  33.8 7.6 %all-to-all-start = ((f32[32,32,1024]{2,1,0:T(8,128)}), f32[32,32,1024]{2,1,0:T(8,128)}, u32[]{:S(2)}, u32[]{:S(2)}) async-start(f32[32,32,1024]{2,1,0:T(8,128)} %stack.38), calls=%async_computation | async-start | bytes 8388608 | tf_op jit(solution)/shard_map/all_to_all | solution.py:78
  41.5 0.7 maximum_bitcast_fusion.6
  42.1 0.7 compare_bitcast_fusion
  42.8 95.1 %all-to-all-done = f32[32,32,1024]{2,1,0:T(8,128)} async-done(((f32[32,32,1024]{2,1,0:T(8,128)}), f32[32,32,1024]{2,1,0:T(8,128)}, u32[]{:S(2)}, u32[]{:S(2)}) %all-to-all-start) | async-done | bytes 4194336 | tf_op jit(solution)/shard_map/all_to_all | solution.py:78
  138.0 3.0 %gather_fusion = f32[64,1024]{1,0:T(8,128)S(1)} fusion(f32[1024,1024]{1,0:T(8,128)} %bitcast.25, s32[1024]{0:T(1024)S(1)} %pad_clamp_fusion), kind=kCustom, calls=%fused_computation | custom fusion | bytes 524544 | tf_op jit(solution)/shard_map/gather | solution.py:79
  141.0 0.8 bitcast_select_fusion
  (15 shorter events, 2.7 us)
Async XLA Ops:
  0.0 1.9 %copy-start = (bf16[4,4,32,16,128]{4,3,2,1,0:T(8,128)(2,1)S(1)}, bf16[4,4,32,16,128]{4,3,2,1,0:T(8,128)(2,1)}, u32[]{:S(2)}) copy-start(bf16[4,4,32,16,128]{4,3,2,1,0:T(8,128)(2,1)} %param.4) | copy-start | bytes 6291460
  1.5 12.1 %collective-permute-start = (bf16[1,4,32,16,128]{4,3,2,1,0:T(8,128)(2,1)S(1)}, bf16[1,4,32,16,128]{4,3,2,1,0:T(8,128)(2,1)S(1)}, u32[]{:S(2)}, u32[]{:S(2)}) collective-permute-start(bf16[1,4,32,16,128]{4,3,2,1,0:T(8,128)(2,1)S(1)} %get-tuple-element.8), channel_id=1, source_target_pairs={{0,224},{32,0},{64,32},{96,64},{128,96},{160,128},{192,160},{224,1... | collective-permute-start | bytes 1572872 | tf_op jit(solution)/shard_map/ppermute | solution.py:9
  2.9 20.1 %collective-permute-start.1 = (bf16[4,1,32,16,128]{4,3,2,1,0:T(8,128)(2,1)}, bf16[4,1,32,16,128]{4,3,2,1,0:T(8,128)(2,1)}, u32[]{:S(2)}, u32[]{:S(2)}) collective-permute-start(bf16[4,1,32,16,128]{4,3,2,1,0:T(8,128)(2,1)} %get-tuple-element.12), channel_id=1, source_target_pairs={{0,31},{1,0},{2,1},{3,2},{4,3},{5,4},{6,5},{7,6},{8,7},{9,8},{10,9... | collective-permute-start | bytes 1572872 | tf_op jit(solution)/shard_map/ppermute | solution.py:9
  14.3 2.2 %copy-start.1 = (bf16[2,4,32,64,128]{4,3,2,1,0:T(8,128)(2,1)S(1)}, bf16[2,4,32,64,128]{4,3,2,1,0:T(8,128)(2,1)}, u32[]{:S(2)}) copy-start(bf16[2,4,32,64,128]{4,3,2,1,0:T(8,128)(2,1)} %param.5) | copy-start | bytes 12582916
  25.0 2.2 %copy-start.2 = (bf16[4,2,32,64,128]{4,3,2,1,0:T(8,128)(2,1)S(1)}, bf16[4,2,32,64,128]{4,3,2,1,0:T(8,128)(2,1)}, u32[]{:S(2)}) copy-start(bf16[4,2,32,64,128]{4,3,2,1,0:T(8,128)(2,1)} %param.6) | copy-start | bytes 12582916
  33.8 104.1 %all-to-all-start = ((f32[32,32,1024]{2,1,0:T(8,128)}), f32[32,32,1024]{2,1,0:T(8,128)}, u32[]{:S(2)}, u32[]{:S(2)}) async-start(f32[32,32,1024]{2,1,0:T(8,128)} %stack.38), calls=%async_computation | async-start | bytes 8388608 | tf_op jit(solution)/shard_map/all_to_all | solution.py:78
